TPU v7x, 32 devices: a whole 2x2x4 slice. The times are simulated.
32 devices in a mesh: span: 8 (over z, y), plane: 4 (over x, core).
Axes of the slice: x: 2, y: 2, z: 4, core: 2. Of those that a mesh axis runs over, the one named last changes fastest.
Arguments:
- adjoint: float32 [3, 32, 81, 512], P(None, 'span', None, 'plane'), may hold values from -6 to 6
- checkpoints: bfloat16 [8, 2, 32, 81, 512], P(None, None, 'span', None, 'plane'), may hold values from -4 to 4
- checkpoint_step: int32 [3], replicated, may hold values from 0 to 7
- metric: float32 [2, 512], P(None, 'plane'), may hold values from 0.004 to 0.016
- helmholtz_inverse: float32 [32, 81, 81], P('span'), may hold values from -0.08 to 0.8
- wall_element: int32 [1024, 2], replicated, may hold values from 0 to 511
- wall_local: int32 [1024, 2], replicated, may hold values from 0 to 80
- wall_weight: float32 [32, 1024], P('span'), may hold values from 0.7 to 140
Outputs:
- adjoint_next: float32 [3, 32, 81, 512], P(None, 'span', None, 'plane')
- control_gradient: float32 [32, 1024], P('span', 'plane')
All inputs are finite; a program needn't handle non-finite values.
Results may differ from a plain program's by a relative error of at most 0.00065.
Values may be sent and summed in bfloat16 or wider, within the bound.
A program may use at most 128 MiB of HBM per device.

v0:
```python
import jax
import jax.numpy as jnp
import numpy as np
from jax import lax
from jax.sharding import PartitionSpec as P

P_SIZE = 8
NSTEP = 3
HIGHEST = lax.Precision.HIGHEST


def chebyshev_matrix(degree):
    points = np.arange(degree + 1)
    abscissa = np.cos(np.pi * points / degree)
    signed = np.where((points == 0) | (points == degree), 2.0, 1.0) * (-1.0) ** points
    spacing = abscissa[:, None] - abscissa[None, :] + np.eye(degree + 1)
    matrix = signed[:, None] / signed[None, :] / spacing
    return matrix - np.eye(degree + 1) * np.sum(matrix, axis=1)[:, None]


def fourier_table(length):
    row_index = np.arange(length)[:, None]
    column = np.arange(length)[None, :]
    wavenumber = (row_index + 1) // 2
    phase_angle = 2.0 * np.pi * wavenumber * column / length
    parity = row_index % 2
    base_rows = np.where(
        row_index == 0, 1.0, np.where(parity == 1, np.cos(phase_angle), np.sin(phase_angle))
    )
    row_scale = np.where(
        (row_index == 0) | (row_index == length - 1), 1.0 / np.sqrt(length), np.sqrt(2.0 / length)
    )
    return base_rows * row_scale


def transport(field_data, velocity, metric):
    side_nodes = P_SIZE + 1
    matrix = jnp.asarray(chebyshev_matrix(P_SIZE), jnp.float32)
    shaped = field_data.reshape(
        field_data.shape[0], field_data.shape[1], side_nodes, side_nodes, field_data.shape[3]
    )
    first_dir = jnp.einsum("ai,czibe->czabe", matrix, shaped, precision=HIGHEST).reshape(
        field_data.shape
    )
    second_dir = jnp.einsum("bi,czaie->czabe", matrix, shaped, precision=HIGHEST).reshape(
        field_data.shape
    )
    speed_data = velocity.astype(jnp.float32)
    return (
        field_data
        + speed_data[0] * (metric[0] * first_dir)
        + speed_data[1] * (metric[1] * second_dir)
    )


def forward_modes(gathered):
    basis_table = jnp.asarray(fourier_table(gathered.shape[1]), jnp.float32)
    return jnp.einsum("jz,czqe->cjqe", basis_table, gathered, precision=HIGHEST)


def backward_planes(solved):
    basis_table = jnp.asarray(fourier_table(solved.shape[1]), jnp.float32)
    return jnp.einsum("jz,cjqe->czqe", basis_table, solved, precision=HIGHEST)


def solve_modes(inverse_block, coefficients):
    return jnp.einsum("jqr,cjre->cjqe", inverse_block, coefficients, precision=HIGHEST)


def to_plane_layout(point_data):
    return lax.all_to_all(point_data, "span", split_axis=1, concat_axis=3, tiled=True)


def wall_terms(field_one, speed_one, flat_index, inside, wall_count):
    rows = field_one.shape[0]
    values = jnp.take(field_one.reshape(rows, -1), flat_index, axis=1)
    speeds = jnp.take(speed_one.reshape(rows, -1), flat_index, axis=1).astype(jnp.float32)
    product = jnp.where(inside, values * speeds, 0.0).reshape(rows, wall_count, 2)
    return jnp.sum(product, axis=2)


def on_device(
    adjoint,
    checkpoints,
    checkpoint_step,
    metric,
    helmholtz_inverse,
    wall_element,
    wall_local,
    wall_weight,
):
    planes_dev = adjoint.shape[1]
    elems_dev = adjoint.shape[3]
    wall_count = wall_element.shape[0]
    span_count = lax.axis_size("span")
    all_modes = lax.all_gather(helmholtz_inverse, "span", axis=0, tiled=True)
    offset = lax.axis_index("plane") * elems_dev
    local_element = wall_element - offset
    inside = ((local_element >= 0) & (local_element < elems_dev)).reshape(-1)
    flat_index = (wall_local * elems_dev + jnp.clip(local_element, 0, elems_dev - 1)).reshape(-1)
    partial_sum = jnp.zeros((planes_dev, wall_count), jnp.float32)
    for substep in range(NSTEP):
        velocity = lax.dynamic_index_in_dim(
            checkpoints, checkpoint_step[substep], 0, keepdims=False
        )
        advected = transport(adjoint, velocity, metric)
        point_data = backward_planes(
            solve_modes(
                all_modes,
                forward_modes(
                    lax.all_to_all(advected, "span", split_axis=3, concat_axis=1, tiled=True)
                ),
            )
        )
        adjoint = to_plane_layout(point_data)
        partial_sum = partial_sum + wall_terms(
            adjoint[1], velocity[1], flat_index, inside, wall_count
        )
    weighted = wall_weight * partial_sum
    grad_share = lax.psum_scatter(weighted, "plane", scatter_dimension=1, tiled=True)
    square_total = lax.psum(jnp.sum(grad_share * grad_share), ("span", "plane"))
    inverse_rms = lax.rsqrt(square_total / (planes_dev * span_count * wall_count) + 1e-06)
    return (adjoint, grad_share * inverse_rms)


def solution(mesh):
    placed = (
        P(None, "span", None, "plane"),
        P(None, None, "span", None, "plane"),
        P(),
        P(None, "plane"),
        P("span", None, None),
        P(),
        P(),
        P("span", None),
    )
    return jax.shard_map(
        on_device,
        mesh=mesh,
        in_specs=placed,
        out_specs=(P(None, "span", None, "plane"), P("span", "plane")),
        check_vma=False,
    )
```

profile of v0, /device:TPU:0, one launch (start us, length us, event | category | flops | bytes accessed | tf_op | source)
XLA Modules:
  0.0 388.5 jit_solution(4690724075645304346)
XLA Ops:
  20.4 7.3 %all-to-all-start = ((f32[3,4,81,128]{2,1,0,3:T(4,128)}), f32[3,4,81,128]{2,1,0,3:T(4,128)S(1)}, u32[]{:S(2)}, u32[]{:S(2)}) async-start(f32[3,4,81,128]{2,1,0,3:T(4,128)} %copy.127), calls=%async_computation | async-start | bytes 1572864 | tf_op jit(solution)/shard_map/all_to_all | solution.py:111
  27.8 47.5 %all_gather.3 = f32[32,81,81]{2,1,0:T(8,128)S(1)} all-gather(f32[4,81,81]{2,1,0:T(8,128)S(1)} %copy.131), channel_id=1, replica_groups=mesh['span'=8,'plane'=4] {'span'}, dimensions={0}, use_global_device_ids=true | all-gather | bytes 944784 | tf_op jit(solution)/shard_map/all_gather | solution.py:96
  82.1 4.0 %all-to-all-start.1 = ((f32[3,32,81,16]{2,3,0,1:T(8,128)}), f32[3,32,81,16]{2,3,0,1:T(8,128)S(1)}, u32[]{:S(2)}, u32[]{:S(2)}) async-start(f32[3,32,81,16]{2,3,0,1:T(8,128)} %copy.135), calls=%async_computation.1 | async-start | bytes 1572864 | tf_op jit(solution)/shard_map/all_to_all | solution.py:71
  86.9 15.1 %all-to-all-done.1 = f32[3,32,81,16]{2,3,0,1:T(8,128)S(1)} async-done(((f32[3,32,81,16]{2,3,0,1:T(8,128)}), f32[3,32,81,16]{2,3,0,1:T(8,128)S(1)}, u32[]{:S(2)}, u32[]{:S(2)}) %all-to-all-start.1) | async-done | bytes 497696 | tf_op jit(solution)/shard_map/all_to_all | solution.py:71
  105.0 3.2 reshape.90
  116.9 21.5 %all_to_all.108 = f32[3,4,81,128]{2,1,0,3:T(4,128)S(1)} all-to-all(f32[3,4,81,128]{2,1,0,3:T(4,128)S(1)} %copy.143), channel_id=1, replica_groups=mesh['span'=8,'plane'=4] {'span'}, dimensions={3} | all-to-all | bytes 995328 | tf_op jit(solution)/shard_map/all_to_all | solution.py:111
  144.4 22.6 %all_to_all.109 = f32[3,32,81,16]{2,3,0,1:T(8,128)S(1)} all-to-all(f32[3,32,81,16]{2,3,0,1:T(8,128)S(1)} %copy.150), channel_id=1, replica_groups=mesh['span'=8,'plane'=4] {'span'}, dimensions={1} | all-to-all | bytes 995328 | tf_op jit(solution)/shard_map/all_to_all | solution.py:71
  167.0 3.1 copy.151
  170.1 3.2 reshape.93
  182.7 3.6 all-to-all-start.4
  186.3 19.8 %all-to-all-done.4 = f32[3,4,81,128]{2,1,0,3:T(4,128)S(1)} async-done(((f32[3,4,81,128]{2,1,0,3:T(4,128)}), f32[3,4,81,128]{2,1,0,3:T(4,128)S(1)}, u32[]{:S(2)}, u32[]{:S(2)}) %all-to-all-start.4) | async-done | bytes 497696 | tf_op jit(solution)/shard_map/all_to_all | solution.py:111
  212.5 3.5 all-to-all-start.5
  223.3 7.7 %gather_fusion.3 = bf16[2048,4]{1,0:T(8,128)(2,1)S(1)} fusion(bf16[4,10368]{0,1:T(8,128)(2,1)} %bitcast.184, s32[2048]{0:T(1024)S(1)} %fusion.33), kind=kCustom, calls=%fused_computation.4.clone | custom fusion | bytes 40960 | tf_op jit(solution)/shard_map/jit(_take)/gather | solution.py:77
  231.0 9.7 %gather_fusion.5 = bf16[2048,4]{1,0:T(8,128)(2,1)} fusion(bf16[4,10368]{0,1:T(8,128)(2,1)} %bitcast.185, s32[2048]{0:T(1024)S(1)} %fusion.33), kind=kCustom, calls=%fused_computation.5.clone | custom fusion | bytes 40960 | tf_op jit(solution)/shard_map/jit(_take)/gather | solution.py:77
  243.1 9.8 %gather_fusion.1 = bf16[2048,4]{1,0:T(8,128)(2,1)} fusion(bf16[4,10368]{0,1:T(8,128)(2,1)} %bitcast.186, s32[2048]{0:T(1024)S(1)} %fusion.33), kind=kCustom, calls=%fused_computation.1.clone | custom fusion | bytes 40960 | tf_op jit(solution)/shard_map/jit(_take)/gather | solution.py:77
  254.3 5.3 %copy.169 = f32[1,4,81,8,16]{1,4,3,2,0:T(8,128)} copy(f32[1,4,81,8,16]{4,3,1,2,0:T(8,128)S(1)} %slice.102) | data formatting | bytes 331776 | tf_op jit(solution)/shard_map/slice | solution.py:117
  259.6 10.1 %gather_fusion = f32[2048,4]{1,0:T(8,128)} fusion(f32[4,10368]{0,1:T(8,128)} %bitcast.167, s32[2048]{0:T(1024)S(1)} %fusion.33), kind=kCustom, calls=%fused_computation.clone | custom fusion | bytes 73728 | tf_op jit(solution)/shard_map/jit(_take)/gather | solution.py:76
  271.1 5.3 %copy.171 = f32[1,4,81,8,16]{1,4,3,2,0:T(8,128)} copy(f32[1,4,81,8,16]{4,3,1,2,0:T(8,128)S(1)} %slice.103) | data formatting | bytes 331776 | tf_op jit(solution)/shard_map/slice | solution.py:117
  276.4 10.1 %gather_fusion.2 = f32[2048,4]{1,0:T(8,128)} fusion(f32[4,10368]{0,1:T(8,128)} %bitcast.168, s32[2048]{0:T(1024)S(1)} %fusion.33), kind=kCustom, calls=%fused_computation.2.clone | custom fusion | bytes 73728 | tf_op jit(solution)/shard_map/jit(_take)/gather | solution.py:76
  286.6 5.7 %copy.173 = f32[1,4,81,8,16]{1,4,3,2,0:T(8,128)} copy(f32[1,4,81,8,16]{2,4,3,1,0:T(8,128)S(1)} %slice.104) | data formatting | bytes 331776 | tf_op jit(solution)/shard_map/slice | solution.py:117
  292.3 10.1 %gather_fusion.4 = f32[2048,4]{1,0:T(8,128)} fusion(f32[4,10368]{0,1:T(8,128)} %bitcast.169, s32[2048]{0:T(1024)S(1)} %fusion.33), kind=kCustom, calls=%fused_computation.3.clone | custom fusion | bytes 73728 | tf_op jit(solution)/shard_map/jit(_take)/gather | solution.py:76
  302.3 4.6 %fusion.16 = (f32[4,2048]{0,1:T(8,128)}, f32[4,2048]{0,1:T(8,128)S(1)}, f32[4,2048]{0,1:T(8,128)S(1)}) fusion(f32[2048,4]{1,0:T(8,128)} %gather_fusion.2, bf16[2048,4]{1,0:T(8,128)(2,1)S(1)} %gather_fusion.3, pred[2048]{0:T(1024)(128)(4,1)S(1)} %compare_and_fusion.1, pred[2048]{0:T(1024)(128)(4,1)S(1)} %reshape.96, bf16[2048,4]{1,0:T(8,128)(2,1)} %gather_fusion.5, ...), kind=kLoop, calls=%fused_computation.30 | loop fusion | flops 122880 | bytes 249856 | tf_op jit(solution)/shard_map/jit(_where)/select_n | solution.py:78
  314.9 23.1 %reduce-scatter.4.cloned.1.call-done = f32[256,4]{1,0:T(8,128)} async-done(((f32[1024,4]{1,0:T(8,128)}), f32[256,4]{1,0:T(8,128)}) %reduce-scatter.4.cloned.1.call-update) | async-done | bytes 4112
  340.6 39.5 %psum.7 = f32[]{:T(128)} all-reduce(f32[]{:T(128)} %multiply_reduce_fusion), channel_id=1, replica_groups=mesh['span'=8,'plane'=4] {'span','plane'}, use_global_device_ids=true, to_apply=%region_5.8 | all-reduce | flops 1 | bytes 8 | tf_op jit(solution)/shard_map/psum | solution.py:121
  (128 shorter events, 71.8 us)
Async XLA Ops:
  7.2 7.4 %copy-start.13 = (f32[9,9,1,1,1]{1,0,4,3,2:T(8,128)S(1)}, f32[9,9,1,1,1]{1,0,4,3,2:T(8,128)}, u32[]{:S(2)}) copy-start(f32[9,9,1,1,1]{1,0,4,3,2:T(8,128)} %constant.58) | copy-start | bytes 976
  7.2 7.4 %copy-start = (f32[3,4,81,128]{3,1,2,0:T(4,128)S(1)}, f32[3,4,81,128]{3,1,2,0:T(4,128)}, u32[]{:S(2)}) copy-start(f32[3,4,81,128]{3,1,2,0:T(4,128)} %param.21) | copy-start | bytes 1492996
  12.6 2.8 copy-start.24
  15.4 3.6 copy-start.18
  15.4 3.6 copy-start.21
  19.3 8.5 %copy-start.14 = (f32[4,81,81]{2,0,1:T(4,128)S(1)}, f32[4,81,81]{2,0,1:T(4,128)}, u32[]{:S(2)}) copy-start(f32[4,81,81]{2,0,1:T(4,128)} %param.25) | copy-start | bytes 314932
  20.4 54.8 %all-to-all-start = ((f32[3,4,81,128]{2,1,0,3:T(4,128)}), f32[3,4,81,128]{2,1,0,3:T(4,128)S(1)}, u32[]{:S(2)}, u32[]{:S(2)}) async-start(f32[3,4,81,128]{2,1,0,3:T(4,128)} %copy.127), calls=%async_computation | async-start | bytes 1572864 | tf_op jit(solution)/shard_map/all_to_all | solution.py:111
  82.1 19.9 %all-to-all-start.1 = ((f32[3,32,81,16]{2,3,0,1:T(8,128)}), f32[3,32,81,16]{2,3,0,1:T(8,128)S(1)}, u32[]{:S(2)}, u32[]{:S(2)}) async-start(f32[3,32,81,16]{2,3,0,1:T(8,128)} %copy.135), calls=%async_computation.1 | async-start | bytes 1572864 | tf_op jit(solution)/shard_map/all_to_all | solution.py:71
  111.8 3.3 copy-start.4
  112.8 2.5 copy-start.2
  115.1 1.1 copy-start.8
  115.1 1.1 copy-start.9
  115.1 1.1 copy-start.19
  115.1 1.1 copy-start.22
  176.9 3.3 copy-start.3
  177.9 2.5 copy-start.1
  180.2 1.0 copy-start.23
  182.7 23.4 %all-to-all-start.4 = ((f32[3,4,81,128]{2,1,0,3:T(4,128)}), f32[3,4,81,128]{2,1,0,3:T(4,128)S(1)}, u32[]{:S(2)}, u32[]{:S(2)}) async-start(f32[3,4,81,128]{2,1,0,3:T(4,128)} %copy.158), calls=%async_computation.4 | async-start | bytes 1572864 | tf_op jit(solution)/shard_map/all_to_all | solution.py:111
  186.3 20.0 %copy-start.12 = (f32[32,32,1,1]{1,0,3,2:T(8,128)S(1)}, f32[32,32,1,1]{1,0,3,2:T(8,128)}, u32[]{:S(2)}) copy-start(f32[32,32,1,1]{1,0,3,2:T(8,128)} %constant.59) | copy-start | bytes 12292
  211.1 5.0 %copy-start.15 = (s32[1024,2]{0,1:T(2,128)S(1)}, s32[1024,2]{0,1:T(2,128)}, u32[]{:S(2)}) copy-start(s32[1024,2]{0,1:T(2,128)} %param.26) | copy-start | bytes 24580
  211.1 5.7 %copy-start.17 = (s32[1024,2]{0,1:T(2,128)S(1)}, s32[1024,2]{0,1:T(2,128)}, u32[]{:S(2)}) copy-start(s32[1024,2]{0,1:T(2,128)} %param.27) | copy-start | bytes 24580
  212.5 74.0 %all-to-all-start.5 = ((f32[3,32,81,16]{2,3,0,1:T(8,128)}), f32[3,32,81,16]{2,3,0,1:T(8,128)S(1)}, u32[]{:S(2)}, u32[]{:S(2)}) async-start(f32[3,32,81,16]{2,3,0,1:T(8,128)} %copy.165), calls=%async_computation.5 | async-start | bytes 1572864 | tf_op jit(solution)/shard_map/all_to_all | solution.py:71
  216.0 121.9 %reduce-scatter.4.cloned.1.call-start = ((), (), s32[]{:S(2)}) async-start(), calls=%async_computation.7 | async-start | bytes 655360
  311.8 1.3 copy-start.5
  (6 other events, 5.3 us)
Sparse Core Ops, SparseCore 0:
  315.0 22.9 reduce-scatter.3
where the time goes:
time: 396 us; the launch traced here: 388 us
  blocking collectives  131 us (33%)
  local copies, waits for them, and re-layouts  121 us (31%)
  waiting for transfers between devices  58 us (15%)
  matrix products  24.4 us (6%)
  between operations  21.5 us (5%)
  starting transfers between devices  18.5 us (5%)
  other arithmetic  13.9 us (4%)
    all_gather x1, blocking collectives, on_device(): all_modes = lax.all_gather(helmholtz_inverse, 'span', axis=0, tiled=True)  47.5 us
    psum x1, blocking collectives, on_device(): square_total = lax.psum(jnp.sum(grad_share * grad_share), ('span', 'plane'))  39.5 us
    gather x3, local copies, waits for them, and re-layouts, wall_terms(): values = jnp.take(field_one.reshape(rows, -1), flat_index, axis=1)  30.2 us
    gather x3, local copies, waits for them, and re-layouts, wall_terms(): jnp.take(speed_one.reshape(rows, -1), flat_index, axis=1)  27.2 us
    unnamed x2, waiting for transfers between devices  23.1 us
    all_to_all x1, blocking collectives, to_plane_layout(): lax.all_to_all(point_data, 'span', split_axis=1, concat_axis=3, tiled=True)  22.6 us
    all_to_all x1, blocking collectives, on_device(): lax.all_to_all(advected, 'span', split_axis=3, concat_axis=1, tiled=True)  21.5 us
    all_to_all x2, waiting for transfers between devices, on_device(): lax.all_to_all(advected, 'span', split_axis=3, concat_axis=1, tiled=True)  19.8 us
  transfers between devices with their start and end apart: 5, of which 3 were waited for; matrix products, arithmetic and copies ran while one was open for 18% of the time, Pallas kernels for 0%

commit v1 on v0

--- a/solution.py
+++ b/solution.py
@@ -7,6 +7,22 @@
 P_SIZE = 8
 NSTEP = 3
 HIGHEST = lax.Precision.HIGHEST
+
+
+def pairwise_exchange(x, axis, split, join):
+    ways, here = (lax.axis_size(axis), lax.axis_index(axis))
+    width = x.shape[split] // ways
+    dims = list(x.shape)
+    dims[split] = width
+    height = dims[join]
+    dims[join] = height * ways
+    full = jnp.zeros(dims, x.dtype)
+    for mask in range(ways):
+        part = lax.dynamic_slice_in_dim(x, (here ^ mask) * width, width, axis=split)
+        if mask:
+            part = lax.ppermute(part, axis, [(d, d ^ mask) for d in range(ways)])
+        full = lax.dynamic_update_slice_in_dim(full, part, (here ^ mask) * height, axis=join)
+    return full
 
 
 def chebyshev_matrix(degree):
@@ -105,12 +121,7 @@
         )
         advected = transport(adjoint, velocity, metric)
         point_data = backward_planes(
-            solve_modes(
-                all_modes,
-                forward_modes(
-                    lax.all_to_all(advected, "span", split_axis=3, concat_axis=1, tiled=True)
-                ),
-            )
+            solve_modes(all_modes, forward_modes(pairwise_exchange(advected, "span", 3, 1)))
         )
         adjoint = to_plane_layout(point_data)
         partial_sum = partial_sum + wall_terms(

time: 396 us -> 626 us (1.58)
  waiting for transfers between devices: 58 us -> 204 us
  local copies, waits for them, and re-layouts: 121 us -> 157 us
  starting transfers between devices: 18.5 us -> 48.3 us
  blocking collectives: 131 us -> 147 us
    ppermute x0 -> x21, waiting for transfers between devices: none -> 154 us  [pairwise_exchange(): part = lax.ppermute(part, axis, [(d, d ^ mask) for d in range(ways)])]
    all_gather x1, blocking collectives: 47.5 us -> 107 us  [on_device(): all_modes = lax.all_gather(helmholtz_inverse, 'span', axis=0, tiled=True)]
    all_to_all x2 -> x0, blocking collectives: 44.2 us -> none  [the longest x1 22.6 us: to_plane_layout(): lax.all_to_all(point_data, 'span', split_axis=1, concat_axis=3, tiled=True)]
    ppermute x0 -> x21, starting transfers between devices: none -> 36.8 us  [pairwise_exchange(): part = lax.ppermute(part, axis, [(d, d ^ mask) for d in range(ways)])]
    ppermute x0 -> x21, local copies, waits for them, and re-layouts: none -> 25.6 us  [pairwise_exchange(): part = lax.ppermute(part, axis, [(d, d ^ mask) for d in range(ways)])]
    all_to_all x2 -> x0, waiting for transfers between devices: 19.8 us -> none  [on_device(): lax.all_to_all(advected, 'span', split_axis=3, concat_axis=1, tiled=True)]
    dynamic_slice x0 -> x6, local copies, waits for them, and re-layouts: none -> 11.7 us  [pairwise_exchange(): part = lax.dynamic_slice_in_dim(x, (here ^ mask) * width, width, axis=split)]
    all_to_all x2 -> x0, starting transfers between devices: 10.9 us -> none  [on_device(): lax.all_to_all(advected, 'span', split_axis=3, concat_axis=1, tiled=True)]
  transfers between devices with their start and end apart: 5 -> 25, of which waited for: 3 -> 11; matrix products, arithmetic and copies ran while one was open for 18% -> 15% of each run, Pallas kernels for 0% -> 0%
where the time goes in v1:
time: 626 us; the launch traced here: 615 us
  waiting for transfers between devices  204 us (33%)
  local copies, waits for them, and re-layouts  157 us (25%)
  blocking collectives  147 us (23%)
  starting transfers between devices  48.3 us (8%)
  matrix products  23.5 us (4%)
  between operations  21.9 us (3%)
  other arithmetic  13.9 us (2%)
    ppermute x21, waiting for transfers between devices, pairwise_exchange(): part = lax.ppermute(part, axis, [(d, d ^ mask) for d in range(ways)])  154 us
    all_gather x1, blocking collectives, on_device(): all_modes = lax.all_gather(helmholtz_inverse, 'span', axis=0, tiled=True)  107 us
    psum x1, blocking collectives, on_device(): square_total = lax.psum(jnp.sum(grad_share * grad_share), ('span', 'plane'))  39.5 us
    ppermute x21, starting transfers between devices, pairwise_exchange(): part = lax.ppermute(part, axis, [(d, d ^ mask) for d in range(ways)])  36.8 us
    gather x3, local copies, waits for them, and re-layouts, wall_terms(): values = jnp.take(field_one.reshape(rows, -1), flat_index, axis=1)  30.2 us
    gather x3, local copies, waits for them, and re-layouts, wall_terms(): jnp.take(speed_one.reshape(rows, -1), flat_index, axis=1)  27.1 us
    all_to_all x3, waiting for transfers between devices, to_plane_layout(): lax.all_to_all(point_data, 'span', split_axis=1, concat_axis=3, tiled=True)  25.7 us
    ppermute x21, local copies, waits for them, and re-layouts, pairwise_exchange(): part = lax.ppermute(part, axis, [(d, d ^ mask) for d in range(ways)])  25.6 us
  transfers between devices with their start and end apart: 25, of which 11 were waited for; matrix products, arithmetic and copies ran while one was open for 15% of the time, Pallas kernels for 0%

profile of v1, /device:TPU:0, one launch (start us, length us, event | category | flops | bytes accessed | tf_op | source)
XLA Modules:
  0.0 615.1 jit_solution(16865341974378185923)
XLA Ops:
  22.9 6.0 collective-permute-start.6
  33.6 107.5 %all_gather.3 = f32[32,81,81]{2,1,0:T(8,128)S(1)} all-gather(f32[4,81,81]{2,1,0:T(8,128)S(1)} %copy.75), channel_id=1, replica_groups=mesh['span'=8,'plane'=4] {'span'}, dimensions={0}, use_global_device_ids=true | all-gather | bytes 944784 | tf_op jit(solution)/shard_map/all_gather | solution.py:112
  142.8 10.9 %collective-permute-done.1 = f32[3,4,81,16]{3,1,2,0:T(4,128)} collective-permute-done((f32[3,4,81,16]{3,1,2,0:T(4,128)}, f32[3,4,81,16]{3,1,2,0:T(4,128)}, u32[]{:S(2)}, u32[]{:S(2)}) %collective-permute-start.1) | collective-permute-done | bytes 62240 | tf_op jit(solution)/shard_map/ppermute | solution.py:23
  154.9 8.8 %collective-permute-done.2 = f32[3,4,81,16]{3,1,2,0:T(4,128)} collective-permute-done((f32[3,4,81,16]{3,1,2,0:T(4,128)}, f32[3,4,81,16]{3,1,2,0:T(4,128)}, u32[]{:S(2)}, u32[]{:S(2)}) %collective-permute-start.2) | collective-permute-done | bytes 62240 | tf_op jit(solution)/shard_map/ppermute | solution.py:23
  180.4 12.4 %all-to-all-done = f32[3,32,81,16]{2,3,0,1:T(8,128)S(1)} async-done(((f32[3,32,81,16]{2,3,0,1:T(8,128)}), f32[3,32,81,16]{2,3,0,1:T(8,128)S(1)}, u32[]{:S(2)}, u32[]{:S(2)}) %all-to-all-start) | async-done | bytes 497696 | tf_op jit(solution)/shard_map/all_to_all | solution.py:87
  220.7 10.5 %collective-permute-done.7 = f32[3,4,81,16]{3,1,2,0:T(4,128)} collective-permute-done((f32[3,4,81,16]{3,1,2,0:T(4,128)}, f32[3,4,81,16]{3,1,2,0:T(4,128)}, u32[]{:S(2)}, u32[]{:S(2)}) %collective-permute-start.7) | collective-permute-done | bytes 62240 | tf_op jit(solution)/shard_map/ppermute | solution.py:23
  232.9 30.7 %collective-permute-done.8 = f32[3,4,81,16]{3,1,2,0:T(4,128)} collective-permute-done((f32[3,4,81,16]{3,1,2,0:T(4,128)}, f32[3,4,81,16]{3,1,2,0:T(4,128)}, u32[]{:S(2)}, u32[]{:S(2)}) %collective-permute-start.8) | collective-permute-done | bytes 62240 | tf_op jit(solution)/shard_map/ppermute | solution.py:23
  267.1 26.8 %collective-permute-done.9 = f32[3,4,81,16]{3,1,2,0:T(4,128)} collective-permute-done((f32[3,4,81,16]{3,1,2,0:T(4,128)}, f32[3,4,81,16]{3,1,2,0:T(4,128)}, u32[]{:S(2)}, u32[]{:S(2)}) %collective-permute-start.9) | collective-permute-done | bytes 62240 | tf_op jit(solution)/shard_map/ppermute | solution.py:23
  310.5 13.3 %all-to-all-done.1 = f32[3,32,81,16]{2,3,0,1:T(8,128)S(1)} async-done(((f32[3,32,81,16]{2,3,0,1:T(8,128)}), f32[3,32,81,16]{2,3,0,1:T(8,128)S(1)}, u32[]{:S(2)}, u32[]{:S(2)}) %all-to-all-start.1) | async-done | bytes 497696 | tf_op jit(solution)/shard_map/all_to_all | solution.py:87
  351.3 10.6 %collective-permute-done.14 = f32[3,4,81,16]{3,1,2,0:T(4,128)} collective-permute-done((f32[3,4,81,16]{3,1,2,0:T(4,128)}, f32[3,4,81,16]{3,1,2,0:T(4,128)}, u32[]{:S(2)}, u32[]{:S(2)}) %collective-permute-start.14) | collective-permute-done | bytes 62240 | tf_op jit(solution)/shard_map/ppermute | solution.py:23
  364.0 29.7 %collective-permute-done.15 = f32[3,4,81,16]{3,1,2,0:T(4,128)} collective-permute-done((f32[3,4,81,16]{3,1,2,0:T(4,128)}, f32[3,4,81,16]{3,1,2,0:T(4,128)}, u32[]{:S(2)}, u32[]{:S(2)}) %collective-permute-start.15) | collective-permute-done | bytes 62240 | tf_op jit(solution)/shard_map/ppermute | solution.py:23
  393.7 4.7 collective-permute-start.16
  399.7 25.9 %collective-permute-done.16 = f32[3,4,81,16]{3,1,2,0:T(4,128)} collective-permute-done((f32[3,4,81,16]{3,1,2,0:T(4,128)}, f32[3,4,81,16]{3,1,2,0:T(4,128)}, u32[]{:S(2)}, u32[]{:S(2)}) %collective-permute-start.16) | collective-permute-done | bytes 62240 | tf_op jit(solution)/shard_map/ppermute | solution.py:23
  448.8 7.7 %gather_fusion.3 = bf16[2048,4]{1,0:T(8,128)(2,1)S(1)} fusion(bf16[4,10368]{0,1:T(8,128)(2,1)} %bitcast.169, s32[2048]{0:T(1024)S(1)} %fusion.30), kind=kCustom, calls=%fused_computation.4.clone | custom fusion | bytes 40960 | tf_op jit(solution)/shard_map/jit(_take)/gather | solution.py:93
  456.4 9.7 %gather_fusion.5 = bf16[2048,4]{1,0:T(8,128)(2,1)} fusion(bf16[4,10368]{0,1:T(8,128)(2,1)} %bitcast.170, s32[2048]{0:T(1024)S(1)} %fusion.30), kind=kCustom, calls=%fused_computation.5.clone | custom fusion | bytes 40960 | tf_op jit(solution)/shard_map/jit(_take)/gather | solution.py:93
  468.6 9.7 %gather_fusion.1 = bf16[2048,4]{1,0:T(8,128)(2,1)} fusion(bf16[4,10368]{0,1:T(8,128)(2,1)} %bitcast.171, s32[2048]{0:T(1024)S(1)} %fusion.30), kind=kCustom, calls=%fused_computation.1.clone | custom fusion | bytes 40960 | tf_op jit(solution)/shard_map/jit(_take)/gather | solution.py:93
  479.7 5.3 copy.121
  485.0 10.1 %gather_fusion = f32[2048,4]{1,0:T(8,128)} fusion(f32[4,10368]{0,1:T(8,128)} %bitcast.158, s32[2048]{0:T(1024)S(1)} %fusion.30), kind=kCustom, calls=%fused_computation.clone | custom fusion | bytes 73728 | tf_op jit(solution)/shard_map/jit(_take)/gather | solution.py:92
  496.5 5.3 copy.123
  501.8 10.1 %gather_fusion.2 = f32[2048,4]{1,0:T(8,128)} fusion(f32[4,10368]{0,1:T(8,128)} %bitcast.159, s32[2048]{0:T(1024)S(1)} %fusion.30), kind=kCustom, calls=%fused_computation.2.clone | custom fusion | bytes 73728 | tf_op jit(solution)/shard_map/jit(_take)/gather | solution.py:92
  512.0 5.7 copy.125
  517.7 10.1 %gather_fusion.4 = f32[2048,4]{1,0:T(8,128)} fusion(f32[4,10368]{0,1:T(8,128)} %bitcast.160, s32[2048]{0:T(1024)S(1)} %fusion.30), kind=kCustom, calls=%fused_computation.3.clone | custom fusion | bytes 73728 | tf_op jit(solution)/shard_map/jit(_take)/gather | solution.py:92
  540.3 24.2 %reduce-scatter.4.cloned.1.call-done = f32[256,4]{1,0:T(8,128)} async-done(((f32[1024,4]{1,0:T(8,128)}), f32[256,4]{1,0:T(8,128)}) %reduce-scatter.4.cloned.1.call-update) | async-done | bytes 4112
  567.1 39.5 %psum.7 = f32[]{:T(128)} all-reduce(f32[]{:T(128)} %multiply_reduce_fusion), channel_id=1, replica_groups=mesh['span'=8,'plane'=4] {'span','plane'}, use_global_device_ids=true, to_apply=%region_5.8 | all-reduce | flops 1 | bytes 8 | tf_op jit(solution)/shard_map/psum | solution.py:132
  (211 shorter events, 158.2 us)
Async XLA Ops:
  22.9 146.0 %collective-permute-start.6 = (f32[3,4,81,16]{3,1,2,0:T(4,128)S(1)}, f32[3,4,81,16]{3,1,2,0:T(4,128)}, u32[]{:S(2)}, u32[]{:S(2)}) collective-permute-start(f32[3,4,81,16]{3,1,2,0:T(4,128)S(1)} %get-tuple-element.32), channel_id=1, source_target_pairs={{0,28},{4,24},{8,20},{12,16},{16,12},{20,8},{24,4},{28,0},{1,29},{... | collective-permute-start | bytes 186632 | tf_op jit(solution)/shard_map/ppermute | solution.py:23
  28.9 138.7 %collective-permute-start.5 = (f32[3,4,81,16]{3,1,2,0:T(4,128)}, f32[3,4,81,16]{3,1,2,0:T(4,128)}, u32[]{:S(2)}, u32[]{:S(2)}) collective-permute-start(f32[3,4,81,16]{3,1,2,0:T(4,128)} %get-tuple-element.33), channel_id=1, source_target_pairs={{0,24},{4,28},{8,16},{12,20},{16,8},{20,12},{24,0},{28,4},{1,25},{... | collective-permute-start | bytes 186632 | tf_op jit(solution)/shard_map/ppermute | solution.py:23
  29.1 137.2 %collective-permute-start.4 = (f32[3,4,81,16]{3,1,2,0:T(4,128)}, f32[3,4,81,16]{3,1,2,0:T(4,128)}, u32[]{:S(2)}, u32[]{:S(2)}) collective-permute-start(f32[3,4,81,16]{3,1,2,0:T(4,128)} %get-tuple-element.34), channel_id=1, source_target_pairs={{0,20},{4,16},{8,28},{12,24},{16,4},{20,0},{24,12},{28,8},{1,21},{... | collective-permute-start | bytes 186632 | tf_op jit(solution)/shard_map/ppermute | solution.py:23
  29.9 135.2 %collective-permute-start.3 = (f32[3,4,81,16]{3,1,2,0:T(4,128)}, f32[3,4,81,16]{3,1,2,0:T(4,128)}, u32[]{:S(2)}, u32[]{:S(2)}) collective-permute-start(f32[3,4,81,16]{3,1,2,0:T(4,128)} %get-tuple-element.35), channel_id=1, source_target_pairs={{0,16},{4,20},{8,24},{12,28},{16,0},{20,4},{24,8},{28,12},{1,17},{... | collective-permute-start | bytes 186632 | tf_op jit(solution)/shard_map/ppermute | solution.py:23
  31.9 109.5 %collective-permute-start = (f32[3,4,81,16]{3,1,2,0:T(4,128)}, f32[3,4,81,16]{3,1,2,0:T(4,128)}, u32[]{:S(2)}, u32[]{:S(2)}) collective-permute-start(f32[3,4,81,16]{3,1,2,0:T(4,128)} %get-tuple-element.38), channel_id=1, source_target_pairs={{0,4},{4,0},{8,12},{12,8},{16,20},{20,16},{24,28},{28,24},{1,5},{5... | collective-permute-start | bytes 186632 | tf_op jit(solution)/shard_map/ppermute | solution.py:23
  141.4 12.2 %collective-permute-start.1 = (f32[3,4,81,16]{3,1,2,0:T(4,128)}, f32[3,4,81,16]{3,1,2,0:T(4,128)}, u32[]{:S(2)}, u32[]{:S(2)}) collective-permute-start(f32[3,4,81,16]{3,1,2,0:T(4,128)} %get-tuple-element.37), channel_id=1, source_target_pairs={{0,8},{4,12},{8,0},{12,4},{16,24},{20,28},{24,16},{28,20},{1,9},{5... | collective-permute-start | bytes 186632 | tf_op jit(solution)/shard_map/ppermute | solution.py:23
  176.1 16.7 %all-to-all-start = ((f32[3,32,81,16]{2,3,0,1:T(8,128)}), f32[3,32,81,16]{2,3,0,1:T(8,128)S(1)}, u32[]{:S(2)}, u32[]{:S(2)}) async-start(f32[3,32,81,16]{2,3,0,1:T(8,128)} %copy.79), calls=%async_computation | async-start | bytes 1572864 | tf_op jit(solution)/shard_map/all_to_all | solution.py:87
  211.6 87.4 %collective-permute-start.13 = (f32[3,4,81,16]{3,1,2,0:T(4,128)S(1)}, f32[3,4,81,16]{3,1,2,0:T(4,128)}, u32[]{:S(2)}, u32[]{:S(2)}) collective-permute-start(f32[3,4,81,16]{3,1,2,0:T(4,128)S(1)} %get-tuple-element.24), channel_id=1, source_target_pairs={{0,28},{4,24},{8,20},{12,16},{16,12},{20,8},{24,4},{28,0},{1,29},{... | collective-permute-start | bytes 186632 | tf_op jit(solution)/shard_map/ppermute | solution.py:23
  213.9 83.8 %collective-permute-start.12 = (f32[3,4,81,16]{3,1,2,0:T(4,128)}, f32[3,4,81,16]{3,1,2,0:T(4,128)}, u32[]{:S(2)}, u32[]{:S(2)}) collective-permute-start(f32[3,4,81,16]{3,1,2,0:T(4,128)} %get-tuple-element.25), channel_id=1, source_target_pairs={{0,24},{4,28},{8,16},{12,20},{16,8},{20,12},{24,0},{28,4},{1,25},{... | collective-permute-start | bytes 186632 | tf_op jit(solution)/shard_map/ppermute | solution.py:23
  216.2 80.2 %collective-permute-start.11 = (f32[3,4,81,16]{3,1,2,0:T(4,128)}, f32[3,4,81,16]{3,1,2,0:T(4,128)}, u32[]{:S(2)}, u32[]{:S(2)}) collective-permute-start(f32[3,4,81,16]{3,1,2,0:T(4,128)} %get-tuple-element.26), channel_id=1, source_target_pairs={{0,20},{4,16},{8,28},{12,24},{16,4},{20,0},{24,12},{28,8},{1,21},{... | collective-permute-start | bytes 186632 | tf_op jit(solution)/shard_map/ppermute | solution.py:23
  216.2 78.9 %collective-permute-start.10 = (f32[3,4,81,16]{3,1,2,0:T(4,128)}, f32[3,4,81,16]{3,1,2,0:T(4,128)}, u32[]{:S(2)}, u32[]{:S(2)}) collective-permute-start(f32[3,4,81,16]{3,1,2,0:T(4,128)} %get-tuple-element.27), channel_id=1, source_target_pairs={{0,16},{4,20},{8,24},{12,28},{16,0},{20,4},{24,8},{28,12},{1,17},{... | collective-permute-start | bytes 186632 | tf_op jit(solution)/shard_map/ppermute | solution.py:23
  219.3 12.0 %collective-permute-start.7 = (f32[3,4,81,16]{3,1,2,0:T(4,128)}, f32[3,4,81,16]{3,1,2,0:T(4,128)}, u32[]{:S(2)}, u32[]{:S(2)}) collective-permute-start(f32[3,4,81,16]{3,1,2,0:T(4,128)} %get-tuple-element.30), channel_id=1, source_target_pairs={{0,4},{4,0},{8,12},{12,8},{16,20},{20,16},{24,28},{28,24},{1,5},{5... | collective-permute-start | bytes 186632 | tf_op jit(solution)/shard_map/ppermute | solution.py:23
  231.3 32.3 %collective-permute-start.8 = (f32[3,4,81,16]{3,1,2,0:T(4,128)}, f32[3,4,81,16]{3,1,2,0:T(4,128)}, u32[]{:S(2)}, u32[]{:S(2)}) collective-permute-start(f32[3,4,81,16]{3,1,2,0:T(4,128)} %get-tuple-element.29), channel_id=1, source_target_pairs={{0,8},{4,12},{8,0},{12,4},{16,24},{20,28},{24,16},{28,20},{1,9},{5... | collective-permute-start | bytes 186632 | tf_op jit(solution)/shard_map/ppermute | solution.py:23
  263.6 30.2 %collective-permute-start.9 = (f32[3,4,81,16]{3,1,2,0:T(4,128)}, f32[3,4,81,16]{3,1,2,0:T(4,128)}, u32[]{:S(2)}, u32[]{:S(2)}) collective-permute-start(f32[3,4,81,16]{3,1,2,0:T(4,128)} %get-tuple-element.28), channel_id=1, source_target_pairs={{0,12},{4,8},{8,4},{12,0},{16,28},{20,24},{24,20},{28,16},{1,13},{... | collective-permute-start | bytes 186632 | tf_op jit(solution)/shard_map/ppermute | solution.py:23
  306.1 17.7 %all-to-all-start.1 = ((f32[3,32,81,16]{2,3,0,1:T(8,128)}), f32[3,32,81,16]{2,3,0,1:T(8,128)S(1)}, u32[]{:S(2)}, u32[]{:S(2)}) async-start(f32[3,32,81,16]{2,3,0,1:T(8,128)} %copy.98), calls=%async_computation.1 | async-start | bytes 1572864 | tf_op jit(solution)/shard_map/all_to_all | solution.py:87
  342.2 88.5 %collective-permute-start.20 = (f32[3,4,81,16]{3,1,2,0:T(4,128)S(1)}, f32[3,4,81,16]{3,1,2,0:T(4,128)}, u32[]{:S(2)}, u32[]{:S(2)}) collective-permute-start(f32[3,4,81,16]{3,1,2,0:T(4,128)S(1)} %get-tuple-element.16), channel_id=1, source_target_pairs={{0,28},{4,24},{8,20},{12,16},{16,12},{20,8},{24,4},{28,0},{1,29},{... | collective-permute-start | bytes 186632 | tf_op jit(solution)/shard_map/ppermute | solution.py:23
  344.4 85.0 %collective-permute-start.19 = (f32[3,4,81,16]{3,1,2,0:T(4,128)S(1)}, f32[3,4,81,16]{3,1,2,0:T(4,128)}, u32[]{:S(2)}, u32[]{:S(2)}) collective-permute-start(f32[3,4,81,16]{3,1,2,0:T(4,128)S(1)} %get-tuple-element.17), channel_id=1, source_target_pairs={{0,24},{4,28},{8,16},{12,20},{16,8},{20,12},{24,0},{28,4},{1,25},{... | collective-permute-start | bytes 186632 | tf_op jit(solution)/shard_map/ppermute | solution.py:23
  346.7 81.4 %collective-permute-start.18 = (f32[3,4,81,16]{3,1,2,0:T(4,128)}, f32[3,4,81,16]{3,1,2,0:T(4,128)}, u32[]{:S(2)}, u32[]{:S(2)}) collective-permute-start(f32[3,4,81,16]{3,1,2,0:T(4,128)} %get-tuple-element.18), channel_id=1, source_target_pairs={{0,20},{4,16},{8,28},{12,24},{16,4},{20,0},{24,12},{28,8},{1,21},{... | collective-permute-start | bytes 186632 | tf_op jit(solution)/shard_map/ppermute | solution.py:23
  346.7 80.1 %collective-permute-start.17 = (f32[3,4,81,16]{3,1,2,0:T(4,128)}, f32[3,4,81,16]{3,1,2,0:T(4,128)}, u32[]{:S(2)}, u32[]{:S(2)}) collective-permute-start(f32[3,4,81,16]{3,1,2,0:T(4,128)} %get-tuple-element.19), channel_id=1, source_target_pairs={{0,16},{4,20},{8,24},{12,28},{16,0},{20,4},{24,8},{28,12},{1,17},{... | collective-permute-start | bytes 186632 | tf_op jit(solution)/shard_map/ppermute | solution.py:23
  349.9 12.0 %collective-permute-start.14 = (f32[3,4,81,16]{3,1,2,0:T(4,128)}, f32[3,4,81,16]{3,1,2,0:T(4,128)}, u32[]{:S(2)}, u32[]{:S(2)}) collective-permute-start(f32[3,4,81,16]{3,1,2,0:T(4,128)} %get-tuple-element.22), channel_id=1, source_target_pairs={{0,4},{4,0},{8,12},{12,8},{16,20},{20,16},{24,28},{28,24},{1,5},{5... | collective-permute-start | bytes 186632 | tf_op jit(solution)/shard_map/ppermute | solution.py:23
  361.9 31.8 %collective-permute-start.15 = (f32[3,4,81,16]{3,1,2,0:T(4,128)}, f32[3,4,81,16]{3,1,2,0:T(4,128)}, u32[]{:S(2)}, u32[]{:S(2)}) collective-permute-start(f32[3,4,81,16]{3,1,2,0:T(4,128)} %get-tuple-element.21), channel_id=1, source_target_pairs={{0,8},{4,12},{8,0},{12,4},{16,24},{20,28},{24,16},{28,20},{1,9},{5... | collective-permute-start | bytes 186632 | tf_op jit(solution)/shard_map/ppermute | solution.py:23
  393.7 31.9 %collective-permute-start.16 = (f32[3,4,81,16]{3,1,2,0:T(4,128)}, f32[3,4,81,16]{3,1,2,0:T(4,128)}, u32[]{:S(2)}, u32[]{:S(2)}) collective-permute-start(f32[3,4,81,16]{3,1,2,0:T(4,128)} %get-tuple-element.20), channel_id=1, source_target_pairs={{0,12},{4,8},{8,4},{12,0},{16,28},{20,24},{24,20},{28,16},{1,13},{... | collective-permute-start | bytes 186632 | tf_op jit(solution)/shard_map/ppermute | solution.py:23
  437.9 74.0 %all-to-all-start.2 = ((f32[3,32,81,16]{2,3,0,1:T(8,128)}), f32[3,32,81,16]{2,3,0,1:T(8,128)S(1)}, u32[]{:S(2)}, u32[]{:S(2)}) async-start(f32[3,32,81,16]{2,3,0,1:T(8,128)} %copy.117), calls=%async_computation.2 | async-start | bytes 1572864 | tf_op jit(solution)/shard_map/all_to_all | solution.py:87
  441.4 123.0 %reduce-scatter.4.cloned.1.call-start = ((), (), s32[]{:S(2)}) async-start(), calls=%async_computation.4 | async-start | bytes 655360
  (26 other events, 97.2 us)
Sparse Core Ops, SparseCore 0:
  540.4 24.0 reduce-scatter.3
